TPU v7x, 32 devices: a whole 2x2x4 slice. The times are simulated.
32 devices in a mesh: sp: 16 (over z, y, x), pb: 2 (over core).
Axes of the slice: x: 2, y: 2, z: 4, core: 2. Of those that a mesh axis runs over, the one named last changes fastest.
Arguments:
- amplitudes: bfloat16 [40, 1024, 1024], P('pb', 'sp'), may hold values from -6 to 6
- virtuals: bfloat16 [1400, 1024], replicated, may hold values from -0.375 to 0.375
- energies: float32 [1024], replicated, may hold values from 0.02 to 0.2
- integrals: bfloat16 [2048, 2048], P('sp'), may hold values from -0.125 to 0.125
- screened: int32 [16, 16], P('sp'), may hold values from 0 to 15, as said below
- counts: int32 [16], P('sp'), may hold values from 1 to 16, 128 in all
- offsets: int32 [2, 16], replicated, may hold values from 0 to 1384
- coupling: bfloat16 [40, 40], P('pb'), may hold values from -1 to 1
Outputs:
- residual: bfloat16 [40, 1024, 1024], P('pb', 'sp')
Inputs may be any that keep to these rules, and one draw needn't show every extreme that they name: `screened`: each row names 16 different blocks.
All inputs are finite; a program needn't handle non-finite values. No bound on the sum of `counts` on one device may be relied on, other than what follows from the above.
Results may differ from a plain program's by a relative error of at most 0.01.
Values may be sent and summed in bfloat16 or wider, within the bound.
No kernel may reach another device: no remote copies, remote signals or barrier semaphores. Data moves between devices by JAX's collectives and lax.ppermute only.
A program may use at most 64 MiB of HBM per device.

v0:
```python
import functools

import jax
import jax.numpy as jnp
from jax import lax
from jax.experimental import pallas as pl
from jax.experimental.pallas import tpu as pltpu
from jax.sharding import PartitionSpec as P

SHELL_ROW = 8
SHELL_COL = 16
WIDTH = SHELL_ROW * SHELL_COL
RIGHT_WIN = 24
LEFT_WIN = 16
LANES = 128
F32 = jnp.float32
BF16 = jnp.bfloat16
VMEM = pl.BlockSpec(memory_space=pltpu.VMEM)
HBM = pl.BlockSpec(memory_space=pltpu.HBM)


def iota(shape, dim):
    return lax.broadcasted_iota(jnp.int32, shape, dim)


def split(index, size):
    return index >> (size.bit_length() - 1), index & (size - 1)


def dot(a, b):
    return jnp.dot(a, b, preferred_element_type=F32)


def dot_t(a, b):
    return lax.dot_general(a, b, (((1,), (1,)), ((), ())), preferred_element_type=F32)


def chunk_of(pairs):
    return max(c for c in (1, 5) if pairs % c == 0)


def window(low, size, nao):
    base = jnp.minimum(low & -8, nao - size)
    return pl.multiple_of(base, 8)


def picks(offs, which, first, count, shell, size, nao):
    cols = count * size
    row, col = iota((shell, cols), 0), iota((shell, cols), 1)
    parts = []
    for t in range(count):
        low = offs[which, first + t]
        delta = low - window(low, size, nao) + t * size
        parts.append(jnp.where(col == row + delta, 1.0, 0.0))
    return jnp.concatenate(parts, axis=0).astype(BF16)


def back_kernel(
    nblk, offs_in, amp, virt, out, right, left, amps,
    offs, right_win, left_win, sems, amp_sems,
):
    pairs, ext_rows, next_ = amp.shape
    nao = virt.shape[0]
    whole = nblk * SHELL_COL
    first = lax.axis_index("sp") * ext_rows
    lane_base = pl.multiple_of(first & -LANES, LANES)
    shift = first - lane_base
    offs_load = pltpu.make_async_copy(offs_in, offs, amp_sems.at[0])
    offs_load.start()
    amp_load = pltpu.make_async_copy(amp, amps, amp_sems.at[1])
    amp_load.start()
    offs_load.wait()
    rights, lefts = [], []
    for b in range(nblk):
        base = window(offs[0, b], LEFT_WIN, nao)
        lefts.append(
            pltpu.make_async_copy(
                virt.at[pl.ds(base, LEFT_WIN), pl.ds(lane_base, LANES)],
                left_win.at[b],
                sems.at[1, b],
            )
        )
        lefts[-1].start()
    for b in range(nblk):
        base = window(offs[1, b], RIGHT_WIN, nao)
        rights.append(
            pltpu.make_async_copy(
                virt.at[pl.ds(base, RIGHT_WIN), :], right_win.at[b], sems.at[0, b]
            )
        )
        rights[-1].start()

    per = LANES // SHELL_COL
    right_picks = [
        picks(offs, 1, t * per, per, SHELL_COL, RIGHT_WIN, nao)
        for t in range(whole // LANES)
    ]
    left_picks = [
        picks(offs, 0, t * per, per, SHELL_ROW, LEFT_WIN, nao) for t in range(whole // LANES)
    ]
    lane_pick = jnp.where(
        iota((ext_rows, LANES), 1) == iota((ext_rows, LANES), 0) + shift, 1.0, 0.0
    ).astype(BF16)
    for load in lefts:
        load.wait()
    left_rows = []
    for t, pick in enumerate(left_picks):
        win = left_win[t * per : (t + 1) * per].reshape(per * LEFT_WIN, LANES)
        wide = dot(pick, win).astype(BF16)
        left[t] = dot_t(lane_pick, wide).astype(BF16)
        left_rows.append(dot_t(wide, lane_pick).astype(BF16))
    for load in rights:
        load.wait()
    for t, pick in enumerate(right_picks):
        win = right_win[t * per : (t + 1) * per].reshape(per * RIGHT_WIN, next_)
        right[t * LANES : (t + 1) * LANES, :] = dot(pick, win).astype(BF16)

    amp_load.wait()
    half = dot_t(amps[...].reshape(pairs * ext_rows, next_), right[...]).astype(BF16)
    side = 2 if pairs % 2 == 0 else 1
    block_of, _ = split(iota((SHELL_ROW, side * LANES), 1) & (LANES - 1), SHELL_COL)
    for q in range(0, pairs, side):
        for t in range(whole // LANES):
            lanes = slice(t * LANES, (t + 1) * LANES)
            beside = jnp.concatenate(
                [half[(q + u) * ext_rows : (q + u + 1) * ext_rows, lanes] for u in range(side)],
                axis=1,
            )
            full = dot(left_rows[t], beside)
            kept = full[:SHELL_ROW]
            for m in range(1, per):
                kept = jnp.where(block_of == m, full[m * SHELL_ROW : (m + 1) * SHELL_ROW], kept)
            for u in range(side):
                rows = slice((q + u) * SHELL_ROW, (q + u + 1) * SHELL_ROW)
                out[rows, lanes] = kept[:, u * LANES : (u + 1) * LANES].astype(BF16)


def ready_kernel(
    nblk, ext_rows, lists_in, live, slab, energies, amps, product, slab_out, lists, slab_in, sems
):
    load = pltpu.make_async_copy(lists_in, lists, sems.at[0])
    load.start()
    slab_load = pltpu.make_async_copy(slab, slab_in, sems.at[1])
    slab_load.start()
    first = lax.axis_index("sp") * ext_rows
    lane_base = pl.multiple_of(first & -LANES, LANES)
    near = energies[:, pl.ds(lane_base, LANES)]
    own = iota((ext_rows, LANES), 1) == iota((ext_rows, LANES), 0) + (first - lane_base)
    own_e = jnp.sum(jnp.where(own, near, 0.0), axis=1, keepdims=True)
    diag = own_e + energies[...]
    for q in range(amps.shape[0]):
        product[q] = diag * amps[q].astype(F32)
    slots = lists.shape[1]
    if slots < nblk:
        slab_out[...] = jnp.zeros(slab_out.shape, BF16)
    count = live[...]
    load.wait()
    slab_load.wait()
    for k in range(slots):
        to = pl.ds(pl.multiple_of(lists[0, k] * WIDTH, WIDTH), WIDTH)
        kept = jnp.where(k < count, slab_in[:, k * WIDTH : (k + 1) * WIDTH].astype(F32), 0.0)
        slab_out[:, to] = kept.astype(BF16)


def regroup(tiles):
    per = len(tiles)
    group, _ = split(iota(tiles[0].shape, 1), SHELL_COL)
    turned = [
        [pltpu.roll(tile, turn * SHELL_COL, 1) if turn else tile for turn in range(per)]
        for tile in tiles
    ]
    pieces = []
    for m in range(per):
        piece = turned[0][-m % per]
        for i in range(1, per):
            piece = jnp.where(group == i, turned[i][(i - m) % per], piece)
        pieces.append(piece)
    return pieces


def add_up(parts):
    total = parts[0][...].astype(F32)
    for part in parts[1:]:
        total = total + part[...].astype(F32)
    return total


def sum_kernel(*refs):
    refs[-1][...] = add_up(refs[:-1]).astype(BF16)


def raw_kernel(pairs, slab, *refs):
    parts, out, ao = refs[:-2], refs[-2], refs[-1]
    total = add_up(parts)
    laid = []
    for t in range(ao.shape[0]):
        ao[t] = total[:, t * LANES : (t + 1) * LANES]
        laid += regroup([ao[t, pl.ds(i, pairs, stride=SHELL_ROW), :] for i in range(SHELL_ROW)])
    raw = dot_t(jnp.concatenate(laid, axis=1).astype(BF16), slab[...]).astype(BF16)
    for d in range(out.shape[0]):
        out[d] = raw


def residual_kernel(
    nblk, halves, chunk, raws, coupling, left, right, product, out, mixed, upper, result, sems
):
    pairs = raws.shape[1]
    ext_rows, next_ = product.shape[1:]
    every = jnp.concatenate(
        [
            jnp.concatenate([raws[b * halves + h].astype(F32) for b in range(nblk)], axis=1)
            for h in range(halves)
        ],
        axis=0,
    ).astype(BF16)
    coupled = dot(coupling[...], every).astype(BF16).astype(F32)
    per = LANES // SHELL_COL
    for t in range(nblk // per):
        tiles = [
            coupled[:, (t * per + m) * WIDTH : (t * per + m + 1) * WIDTH] for m in range(per)
        ]
        for i, piece in enumerate(regroup(tiles)):
            mixed[t, pl.ds(i, pairs, stride=SHELL_ROW), :] = piece

    side = 2 if pairs % 2 == 0 else 1
    block_of, _ = split(iota((SHELL_ROW, side * LANES), 1) & (LANES - 1), SHELL_COL)
    for q in range(0, pairs, side):
        columns = []
        for t in range(nblk // per):
            squares = jnp.concatenate(
                [mixed[t, (q + u) * SHELL_ROW : (q + u + 1) * SHELL_ROW, :] for u in range(side)],
                axis=1,
            )
            stack = [jnp.where(block_of == m, squares, 0.0) for m in range(per)]
            columns.append(dot(left[t], jnp.concatenate(stack, axis=0).astype(BF16)))
        for u in range(side):
            lanes = slice(u * LANES, (u + 1) * LANES)
            upper[q + u] = jnp.concatenate([x[:, lanes] for x in columns], axis=1).astype(BF16)
    copies = []
    for c in range(pairs // chunk):
        part = pl.ds(c * chunk, chunk)
        flat = upper[part].reshape(chunk * ext_rows, nblk * SHELL_COL)
        inner = dot(flat, right[...]).reshape(chunk, ext_rows, next_)
        result[part] = (inner + product[part]).astype(BF16)
        copies.append(pltpu.make_async_copy(result.at[part], out.at[part], sems.at[c]))
        copies[-1].start()
    for copy in copies:
        copy.wait()


def shards(amplitudes, virtuals, energies, integrals, screened, counts, offsets, coupling):
    pairs, ext_rows, next_ = amplitudes.shape
    nblk = offsets.shape[1]
    n = lax.axis_size("sp")
    halves = lax.axis_size("pb")
    span = nblk * SHELL_COL
    chunk = chunk_of(pairs)
    plain = pltpu.CompilerParams(vmem_limit_bytes=min(60, nblk) * 1024 * 1024)
    in_hbm = functools.partial(
        pltpu.with_memory_space_constraint, memory_space=pltpu.HBM
    )

    partial, right, left, held = pl.pallas_call(
        functools.partial(back_kernel, nblk),
        in_specs=[HBM] * 3,
        out_specs=[VMEM] * 4,
        out_shape=[
            jax.ShapeDtypeStruct((pairs * SHELL_ROW, span), BF16),
            jax.ShapeDtypeStruct((span, next_), BF16),
            jax.ShapeDtypeStruct((span // LANES, ext_rows, LANES // SHELL_COL * SHELL_ROW), BF16),
            jax.ShapeDtypeStruct(amplitudes.shape, BF16),
        ],
        scratch_shapes=[
            pltpu.SMEM(offsets.shape, jnp.int32),
            pltpu.VMEM((nblk, RIGHT_WIN, next_), BF16),
            pltpu.VMEM((nblk, LEFT_WIN, LANES), BF16),
            pltpu.SemaphoreType.DMA((2, nblk)),
            pltpu.SemaphoreType.DMA((3,)),
        ],
        compiler_params=plain,
        name="back",
    )(in_hbm(offsets), in_hbm(amplitudes), in_hbm(virtuals))

    product, slab = pl.pallas_call(
        functools.partial(ready_kernel, nblk, ext_rows),
        in_specs=[HBM, VMEM, HBM, VMEM, VMEM],
        out_specs=[VMEM] * 2,
        out_shape=[
            jax.ShapeDtypeStruct(amplitudes.shape, F32),
            jax.ShapeDtypeStruct((WIDTH, nblk * WIDTH), BF16),
        ],
        scratch_shapes=[
            pltpu.SMEM(screened.shape, jnp.int32),
            pltpu.VMEM(integrals.shape, BF16),
            pltpu.SemaphoreType.DMA((2,)),
        ],
        compiler_params=plain,
        name="ready",
    )(
        in_hbm(screened), counts[None], in_hbm(integrals), energies[None], held
    )

    stages, below = [], 1
    while below < n:
        stages.append((below, 4 if n // below % 4 == 0 else 2))
        below *= stages[-1][1]
    turned = len({radix for _, radix in stages}) == 1

    def peer(step, turn, i, h):
        below, radix = stages[(step + h * turned) % len(stages)]
        digit = i // below % radix
        return i + ((digit ^ turn) - digit) * below

    def reaches(step):
        parts = []
        for turn in range(1, stages[step][1]):
            ring = [
                (i * halves + h, peer(step, turn, i, h) * halves + h)
                for i in range(n)
                for h in range(halves)
            ]
            parts.append(lax.ppermute(partial, ("sp", "pb"), ring))
        return parts

    for step in range(len(stages) - 1):
        parts = [partial] + reaches(step)
        partial = pl.pallas_call(
            sum_kernel,
            in_specs=[VMEM] * len(parts),
            out_specs=VMEM,
            out_shape=jax.ShapeDtypeStruct(partial.shape, BF16),
            compiler_params=plain,
            name="sum",
        )(*parts)
    parts = [partial] + reaches(len(stages) - 1)
    raw = pl.pallas_call(
        functools.partial(raw_kernel, pairs),
        in_specs=[VMEM] * (1 + len(parts)),
        out_specs=VMEM,
        out_shape=jax.ShapeDtypeStruct((n * halves, pairs, WIDTH), BF16),
        scratch_shapes=[pltpu.VMEM((span // LANES, pairs * SHELL_ROW, LANES), F32)],
        compiler_params=plain,
        name="raw",
    )(slab, *parts)

    raws = lax.all_to_all(raw, ("sp", "pb"), 0, 0, tiled=True)
    return pl.pallas_call(
        functools.partial(residual_kernel, nblk, halves, chunk),
        in_specs=[VMEM] * 5,
        out_specs=HBM,
        out_shape=jax.ShapeDtypeStruct(amplitudes.shape, BF16),
        scratch_shapes=[
            pltpu.VMEM((span // LANES, pairs * SHELL_ROW, LANES), F32),
            pltpu.VMEM((pairs, ext_rows, span), BF16),
            pltpu.VMEM(amplitudes.shape, BF16),
            pltpu.SemaphoreType.DMA((pairs // chunk,)),
        ],
        compiler_params=plain,
        name="residual",
    )(raws, coupling, left, right, product)


def solution(mesh):
    return jax.shard_map(
        shards,
        mesh=mesh,
        in_specs=(
            P("pb", "sp", None),
            P(),
            P(),
            P("sp", None),
            P("sp", None),
            P("sp"),
            P(),
            P("pb", None),
        ),
        out_specs=P("pb", "sp", None),
        check_vma=False,
    )
```

profile of v0, /device:TPU:0, one launch (start us, length us, event | category | flops | bytes accessed | tf_op | source)
XLA Modules:
  0.0 38.0 jit_solution(14990398615581070356)
XLA Ops:
  0.0 0.0 copy-start.1
  0.0 4.1 %back.1 = (bf16[160,256]{1,0:T(8,128)(2,1)S(1)}, bf16[256,1024]{1,0:T(8,128)(2,1)S(1)}, bf16[2,64,64]{2,1,0:T(8,128)(2,1)S(1)}, bf16[20,64,1024]{2,1,0:T(8,128)(2,1)S(1)}) custom-call(s32[2,16]{1,0:T(2,128)} %offs_in.1, bf16[20,64,1024]{2,1,0:T(8,128)(2,1)} %amp.1, bf16[1400,1024]{1,0:T(8,128)(2,1)} %virt.1), custom_call_target="tpu_custom_call" | custom-call | tf_op jit(solution)/shard_map/back/pallas_call | solution.py:263
  4.1 0.0 copy-start
  4.1 3.0 %collective-permute-start = (bf16[160,256]{1,0:T(8,128)(2,1)S(1)}, bf16[160,256]{1,0:T(8,128)(2,1)S(1)}, u32[]{:S(2)}, u32[]{:S(2)}) collective-permute-start(bf16[160,256]{1,0:T(8,128)(2,1)S(1)} %get-tuple-element.13.refs_0_), channel_id=1, source_target_pairs={{0,2},{1,9},{2,0},{3,11},{4,6},{5,13},{6,4},{7,15},{8,10},{9,1},{1... | collective-permute-start | bytes 245768 | tf_op jit(solution)/shard_map/ppermute | solution.py:322
  7.2 1.5 %collective-permute-start.1 = (bf16[160,256]{1,0:T(8,128)(2,1)S(1)}, bf16[160,256]{1,0:T(8,128)(2,1)S(1)}, u32[]{:S(2)}, u32[]{:S(2)}) collective-permute-start(bf16[160,256]{1,0:T(8,128)(2,1)S(1)} %get-tuple-element.13.refs_0_), channel_id=1, source_target_pairs={{0,4},{1,17},{2,6},{3,19},{4,0},{5,21},{6,2},{7,23},{8,12},{9,25},... | collective-permute-start | bytes 245768 | tf_op jit(solution)/shard_map/ppermute | solution.py:322
  8.7 0.0 collective-permute-start.2
  8.7 0.9 %collective-permute-done.refs_1_ = bf16[160,256]{1,0:T(8,128)(2,1)S(1)} collective-permute-done((bf16[160,256]{1,0:T(8,128)(2,1)S(1)}, bf16[160,256]{1,0:T(8,128)(2,1)S(1)}, u32[]{:S(2)}, u32[]{:S(2)}) %collective-permute-start) | collective-permute-done | bytes 81952 | tf_op jit(solution)/shard_map/ppermute | solution.py:322
  9.6 2.0 %collective-permute-done.1.refs_2_ = bf16[160,256]{1,0:T(8,128)(2,1)S(1)} collective-permute-done((bf16[160,256]{1,0:T(8,128)(2,1)S(1)}, bf16[160,256]{1,0:T(8,128)(2,1)S(1)}, u32[]{:S(2)}, u32[]{:S(2)}) %collective-permute-start.1) | collective-permute-done | bytes 81952 | tf_op jit(solution)/shard_map/ppermute | solution.py:322
  11.6 2.4 %collective-permute-done.2.refs_3_ = bf16[160,256]{1,0:T(8,128)(2,1)S(1)} collective-permute-done((bf16[160,256]{1,0:T(8,128)(2,1)S(1)}, bf16[160,256]{1,0:T(8,128)(2,1)S(1)}, u32[]{:S(2)}, u32[]{:S(2)}) %collective-permute-start.2) | collective-permute-done | bytes 81952 | tf_op jit(solution)/shard_map/ppermute | solution.py:322
  14.1 1.6 %collective-permute-start.3 = (bf16[160,256]{1,0:T(8,128)(2,1)S(1)}, bf16[160,256]{1,0:T(8,128)(2,1)S(1)}, u32[]{:S(2)}, u32[]{:S(2)}) collective-permute-start(bf16[160,256]{1,0:T(8,128)(2,1)S(1)} %sum.1.refs_0_), channel_id=1, source_target_pairs={{0,8},{1,3},{2,10},{3,1},{4,12},{5,7},{6,14},{7,5},{8,0},{9,11},{1... | collective-permute-start | bytes 245768 | tf_op jit(solution)/shard_map/ppermute | solution.py:322
  15.7 2.6 %collective-permute-start.4 = (bf16[160,256]{1,0:T(8,128)(2,1)S(1)}, bf16[160,256]{1,0:T(8,128)(2,1)S(1)}, u32[]{:S(2)}, u32[]{:S(2)}) collective-permute-start(bf16[160,256]{1,0:T(8,128)(2,1)S(1)} %sum.1.refs_0_), channel_id=1, source_target_pairs={{0,16},{1,5},{2,18},{3,7},{4,20},{5,1},{6,22},{7,3},{8,24},{9,13},... | collective-permute-start | bytes 245768 | tf_op jit(solution)/shard_map/ppermute | solution.py:322
  18.3 0.2 collective-permute-start.5
  19.2 0.0 copy-done.1
  19.2 1.3 %ready.1 = (f32[20,64,1024]{2,1,0:T(8,128)S(1)}, bf16[128,2048]{1,0:T(8,128)(2,1)S(1)}) custom-call(s32[1,16]{1,0:T(1,128)} %lists_in.1, s32[1,1]{1,0:T(1,128)} %bitcast.2.live, bf16[128,2048]{1,0:T(8,128)(2,1)} %slab.1, f32[1,1024]{1,0:T(1,128)S(1)} %bitcast.3, bf16[20,64,1024]{2,1,0:T(8,128)(2,1)S(1)} %get-tuple-element.11.amps), custom_call_target="tpu_custom_call" | custom-call | tf_op jit(solution)/shard_map/ready/pallas_call | solution.py:284
  20.5 0.0 collective-permute-done.3.refs_1_
  20.5 1.4 %collective-permute-done.4.refs_2_ = bf16[160,256]{1,0:T(8,128)(2,1)S(1)} collective-permute-done((bf16[160,256]{1,0:T(8,128)(2,1)S(1)}, bf16[160,256]{1,0:T(8,128)(2,1)S(1)}, u32[]{:S(2)}, u32[]{:S(2)}) %collective-permute-start.4) | collective-permute-done | bytes 81952 | tf_op jit(solution)/shard_map/ppermute | solution.py:322
  21.9 2.6 %collective-permute-done.5.refs_3_ = bf16[160,256]{1,0:T(8,128)(2,1)S(1)} collective-permute-done((bf16[160,256]{1,0:T(8,128)(2,1)S(1)}, bf16[160,256]{1,0:T(8,128)(2,1)S(1)}, u32[]{:S(2)}, u32[]{:S(2)}) %collective-permute-start.5) | collective-permute-done | bytes 81952 | tf_op jit(solution)/shard_map/ppermute | solution.py:322
  24.5 0.4 %raw.1 = bf16[32,20,128]{2,1,0:T(8,128)(2,1)S(1)} custom-call(bf16[128,2048]{1,0:T(8,128)(2,1)S(1)} %get-tuple-element.12.slab, bf16[160,256]{1,0:T(8,128)(2,1)S(1)} %sum.1.refs_0_, bf16[160,256]{1,0:T(8,128)(2,1)S(1)} %collective-permute-done.3.refs_1_, bf16[160,256]{1,0:T(8,128)(2,1)S(1)} %collective-permute-done.4.refs_2_, ...), custom_call_target="tpu_custom_call" | custom-call | tf_op jit(solution)/shard_map/raw/pallas_call | solution.py:336
  25.0 10.7 %all_to_all.5.raws = bf16[32,20,128]{2,1,0:T(8,128)(2,1)S(1)} all-to-all(bf16[32,20,128]{2,1,0:T(8,128)(2,1)S(1)} %raw.1), channel_id=1, replica_groups=mesh['sp'=16,'pb'=2] {'sp','pb'}, dimensions={0} | all-to-all | bytes 327680 | tf_op jit(solution)/shard_map/all_to_all | solution.py:346
  35.6 0.0 copy-done
  35.6 2.3 %residual.1 = bf16[20,64,1024]{2,1,0:T(8,128)(2,1)} custom-call(bf16[32,20,128]{2,1,0:T(8,128)(2,1)S(1)} %all_to_all.5.raws, bf16[20,40]{1,0:T(8,128)(2,1)S(1)} %copy-done, bf16[2,64,64]{2,1,0:T(8,128)(2,1)S(1)} %get-tuple-element.14.left, bf16[256,1024]{1,0:T(8,128)(2,1)S(1)} %get-tuple-element.15.right, f32[20,64,1024]{2,1,0:T(8,128)S(1)} %get-tuple-element.16.product), custom_call_target="tpu_custom_call" | custom-call | tf_op jit(solution)/shard_map/residual/pallas_call | solution.py:347
  (1 shorter events, 0.0 us)
Async XLA Ops:
  0.0 19.2 %copy-start.1 = (f32[1024]{0:T(1024)S(1)}, f32[1024]{0:T(1024)}, u32[]{:S(2)}) copy-start(f32[1024]{0:T(1024)} %param.10) | copy-start | bytes 12292
  4.1 31.5 %copy-start = (bf16[20,40]{1,0:T(8,128)(2,1)S(1)}, bf16[20,40]{1,0:T(8,128)(2,1)}, u32[]{:S(2)}) copy-start(bf16[20,40]{1,0:T(8,128)(2,1)} %coupling.1) | copy-start | bytes 4804
  4.1 5.5 %collective-permute-start = (bf16[160,256]{1,0:T(8,128)(2,1)S(1)}, bf16[160,256]{1,0:T(8,128)(2,1)S(1)}, u32[]{:S(2)}, u32[]{:S(2)}) collective-permute-start(bf16[160,256]{1,0:T(8,128)(2,1)S(1)} %get-tuple-element.13.refs_0_), channel_id=1, source_target_pairs={{0,2},{1,9},{2,0},{3,11},{4,6},{5,13},{6,4},{7,15},{8,10},{9,1},{1... | collective-permute-start | bytes 245768 | tf_op jit(solution)/shard_map/ppermute | solution.py:322
  7.2 4.4 %collective-permute-start.1 = (bf16[160,256]{1,0:T(8,128)(2,1)S(1)}, bf16[160,256]{1,0:T(8,128)(2,1)S(1)}, u32[]{:S(2)}, u32[]{:S(2)}) collective-permute-start(bf16[160,256]{1,0:T(8,128)(2,1)S(1)} %get-tuple-element.13.refs_0_), channel_id=1, source_target_pairs={{0,4},{1,17},{2,6},{3,19},{4,0},{5,21},{6,2},{7,23},{8,12},{9,25},... | collective-permute-start | bytes 245768 | tf_op jit(solution)/shard_map/ppermute | solution.py:322
  8.7 5.3 %collective-permute-start.2 = (bf16[160,256]{1,0:T(8,128)(2,1)S(1)}, bf16[160,256]{1,0:T(8,128)(2,1)S(1)}, u32[]{:S(2)}, u32[]{:S(2)}) collective-permute-start(bf16[160,256]{1,0:T(8,128)(2,1)S(1)} %get-tuple-element.13.refs_0_), channel_id=1, source_target_pairs={{0,6},{1,25},{2,4},{3,27},{4,2},{5,29},{6,0},{7,31},{8,14},{9,17},... | collective-permute-start | bytes 245768 | tf_op jit(solution)/shard_map/ppermute | solution.py:322
  14.1 6.4 %collective-permute-start.3 = (bf16[160,256]{1,0:T(8,128)(2,1)S(1)}, bf16[160,256]{1,0:T(8,128)(2,1)S(1)}, u32[]{:S(2)}, u32[]{:S(2)}) collective-permute-start(bf16[160,256]{1,0:T(8,128)(2,1)S(1)} %sum.1.refs_0_), channel_id=1, source_target_pairs={{0,8},{1,3},{2,10},{3,1},{4,12},{5,7},{6,14},{7,5},{8,0},{9,11},{1... | collective-permute-start | bytes 245768 | tf_op jit(solution)/shard_map/ppermute | solution.py:322
  15.7 6.2 %collective-permute-start.4 = (bf16[160,256]{1,0:T(8,128)(2,1)S(1)}, bf16[160,256]{1,0:T(8,128)(2,1)S(1)}, u32[]{:S(2)}, u32[]{:S(2)}) collective-permute-start(bf16[160,256]{1,0:T(8,128)(2,1)S(1)} %sum.1.refs_0_), channel_id=1, source_target_pairs={{0,16},{1,5},{2,18},{3,7},{4,20},{5,1},{6,22},{7,3},{8,24},{9,13},... | collective-permute-start | bytes 245768 | tf_op jit(solution)/shard_map/ppermute | solution.py:322
  18.3 6.2 %collective-permute-start.5 = (bf16[160,256]{1,0:T(8,128)(2,1)S(1)}, bf16[160,256]{1,0:T(8,128)(2,1)S(1)}, u32[]{:S(2)}, u32[]{:S(2)}) collective-permute-start(bf16[160,256]{1,0:T(8,128)(2,1)S(1)} %sum.1.refs_0_), channel_id=1, source_target_pairs={{0,24},{1,7},{2,26},{3,5},{4,28},{5,3},{6,30},{7,1},{8,16},{9,15},... | collective-permute-start | bytes 245768 | tf_op jit(solution)/shard_map/ppermute | solution.py:322
where the time goes:
time: 38.2 us; the launch traced here: 38 us
  blocking collectives  10.7 us (28%)
  waiting for transfers between devices  9.37 us (25%)
  starting transfers between devices  9.04 us (24%)
  Pallas kernels  8.18 us (21%)
  between operations  0.71 us (2%)
    all_to_all x1, blocking collectives, shards(): raws = lax.all_to_all(raw, ('sp', 'pb'), 0, 0, tiled=True)  10.7 us
    ppermute x6, waiting for transfers between devices, reaches(): parts.append(lax.ppermute(partial, ('sp', 'pb'), ring))  9.37 us
    ppermute x6, starting transfers between devices, reaches(): parts.append(lax.ppermute(partial, ('sp', 'pb'), ring))  9.04 us
    pallas_call x1, Pallas kernels, shards(): pl.pallas_call(functools.partial(back_kernel, nblk), in_specs=[HBM] * 3,...  4.1 us
    pallas_call x1, Pallas kernels, shards(): pl.pallas_call(functools.partial(residual_kernel, nblk, halves, chunk), i...  2.34 us
    pallas_call x1, Pallas kernels, shards(): pl.pallas_call(functools.partial(ready_kernel, nblk, ext_rows), in_specs=...  1.28 us
  transfers between devices with their start and end apart: 6, of which 5 were waited for; matrix products, arithmetic and copies ran while one was open for 0% of the time, Pallas kernels for 3%

commit v1 on v0

--- a/solution.py
+++ b/solution.py
@@ -194,7 +194,7 @@
     total = add_up(parts)
     laid = []
     for t in range(ao.shape[0]):
-        ao[t] = total[:, t * LANES : (t + 1) * LANES]
+        ao[t, : total.shape[0]] = total[:, t * LANES : (t + 1) * LANES]
         laid += regroup([ao[t, pl.ds(i, pairs, stride=SHELL_ROW), :] for i in range(SHELL_ROW)])
     raw = dot_t(jnp.concatenate(laid, axis=1).astype(BF16), slab[...]).astype(BF16)
     for d in range(out.shape[0]):
@@ -255,6 +255,7 @@
     halves = lax.axis_size("pb")
     span = nblk * SHELL_COL
     chunk = chunk_of(pairs)
+    strided = -(-pairs // 8) * 8 * SHELL_ROW
     plain = pltpu.CompilerParams(vmem_limit_bytes=min(60, nblk) * 1024 * 1024)
     in_hbm = functools.partial(
         pltpu.with_memory_space_constraint, memory_space=pltpu.HBM
@@ -338,7 +339,7 @@
         in_specs=[VMEM] * (1 + len(parts)),
         out_specs=VMEM,
         out_shape=jax.ShapeDtypeStruct((n * halves, pairs, WIDTH), BF16),
-        scratch_shapes=[pltpu.VMEM((span // LANES, pairs * SHELL_ROW, LANES), F32)],
+        scratch_shapes=[pltpu.VMEM((span // LANES, strided, LANES), F32)],
         compiler_params=plain,
         name="raw",
     )(slab, *parts)
@@ -350,7 +351,7 @@
         out_specs=HBM,
         out_shape=jax.ShapeDtypeStruct(amplitudes.shape, BF16),
         scratch_shapes=[
-            pltpu.VMEM((span // LANES, pairs * SHELL_ROW, LANES), F32),
+            pltpu.VMEM((span // LANES, strided, LANES), F32),
             pltpu.VMEM((pairs, ext_rows, span), BF16),
             pltpu.VMEM(amplitudes.shape, BF16),
             pltpu.SemaphoreType.DMA((pairs // chunk,)),

time: 38.2 us -> 38.2 us (level)
  no operation moved by 1% of the time
where the time goes in v1:
time: 38.2 us; the launch traced here: 38 us
  blocking collectives  10.7 us (28%)
  waiting for transfers between devices  9.37 us (25%)
  starting transfers between devices  9.04 us (24%)
  Pallas kernels  8.18 us (21%)
  between operations  0.71 us (2%)
    all_to_all x1, blocking collectives, shards(): raws = lax.all_to_all(raw, ('sp', 'pb'), 0, 0, tiled=True)  10.7 us
    ppermute x6, waiting for transfers between devices, reaches(): parts.append(lax.ppermute(partial, ('sp', 'pb'), ring))  9.37 us
    ppermute x6, starting transfers between devices, reaches(): parts.append(lax.ppermute(partial, ('sp', 'pb'), ring))  9.04 us
    pallas_call x1, Pallas kernels, shards(): pl.pallas_call(functools.partial(back_kernel, nblk), in_specs=[HBM] * 3,...  4.1 us
    pallas_call x1, Pallas kernels, shards(): pl.pallas_call(functools.partial(residual_kernel, nblk, halves, chunk), i...  2.34 us
    pallas_call x1, Pallas kernels, shards(): pl.pallas_call(functools.partial(ready_kernel, nblk, ext_rows), in_specs=...  1.28 us
  transfers between devices with their start and end apart: 6, of which 5 were waited for; matrix products, arithmetic and copies ran while one was open for 0% of the time, Pallas kernels for 3%

profile of v1, /device:TPU:0, one launch (start us, length us, event | category | flops | bytes accessed | tf_op | source)
XLA Modules:
  0.0 38.0 jit_solution(11834626474577808028)
XLA Ops:
  0.0 0.0 copy-start.1
  0.0 4.1 %back.1 = (bf16[160,256]{1,0:T(8,128)(2,1)S(1)}, bf16[256,1024]{1,0:T(8,128)(2,1)S(1)}, bf16[2,64,64]{2,1,0:T(8,128)(2,1)S(1)}, bf16[20,64,1024]{2,1,0:T(8,128)(2,1)S(1)}) custom-call(s32[2,16]{1,0:T(2,128)} %offs_in.1, bf16[20,64,1024]{2,1,0:T(8,128)(2,1)} %amp.1, bf16[1400,1024]{1,0:T(8,128)(2,1)} %virt.1), custom_call_target="tpu_custom_call" | custom-call | tf_op jit(solution)/shard_map/back/pallas_call | solution.py:264
  4.1 0.0 copy-start
  4.1 3.0 %collective-permute-start = (bf16[160,256]{1,0:T(8,128)(2,1)S(1)}, bf16[160,256]{1,0:T(8,128)(2,1)S(1)}, u32[]{:S(2)}, u32[]{:S(2)}) collective-permute-start(bf16[160,256]{1,0:T(8,128)(2,1)S(1)} %get-tuple-element.13.refs_0_), channel_id=1, source_target_pairs={{0,2},{1,9},{2,0},{3,11},{4,6},{5,13},{6,4},{7,15},{8,10},{9,1},{1... | collective-permute-start | bytes 245768 | tf_op jit(solution)/shard_map/ppermute | solution.py:323
  7.2 1.5 %collective-permute-start.1 = (bf16[160,256]{1,0:T(8,128)(2,1)S(1)}, bf16[160,256]{1,0:T(8,128)(2,1)S(1)}, u32[]{:S(2)}, u32[]{:S(2)}) collective-permute-start(bf16[160,256]{1,0:T(8,128)(2,1)S(1)} %get-tuple-element.13.refs_0_), channel_id=1, source_target_pairs={{0,4},{1,17},{2,6},{3,19},{4,0},{5,21},{6,2},{7,23},{8,12},{9,25},... | collective-permute-start | bytes 245768 | tf_op jit(solution)/shard_map/ppermute | solution.py:323
  8.7 0.0 collective-permute-start.2
  8.7 0.9 %collective-permute-done.refs_1_ = bf16[160,256]{1,0:T(8,128)(2,1)S(1)} collective-permute-done((bf16[160,256]{1,0:T(8,128)(2,1)S(1)}, bf16[160,256]{1,0:T(8,128)(2,1)S(1)}, u32[]{:S(2)}, u32[]{:S(2)}) %collective-permute-start) | collective-permute-done | bytes 81952 | tf_op jit(solution)/shard_map/ppermute | solution.py:323
  9.6 2.0 %collective-permute-done.1.refs_2_ = bf16[160,256]{1,0:T(8,128)(2,1)S(1)} collective-permute-done((bf16[160,256]{1,0:T(8,128)(2,1)S(1)}, bf16[160,256]{1,0:T(8,128)(2,1)S(1)}, u32[]{:S(2)}, u32[]{:S(2)}) %collective-permute-start.1) | collective-permute-done | bytes 81952 | tf_op jit(solution)/shard_map/ppermute | solution.py:323
  11.6 2.4 %collective-permute-done.2.refs_3_ = bf16[160,256]{1,0:T(8,128)(2,1)S(1)} collective-permute-done((bf16[160,256]{1,0:T(8,128)(2,1)S(1)}, bf16[160,256]{1,0:T(8,128)(2,1)S(1)}, u32[]{:S(2)}, u32[]{:S(2)}) %collective-permute-start.2) | collective-permute-done | bytes 81952 | tf_op jit(solution)/shard_map/ppermute | solution.py:323
  14.1 1.6 %collective-permute-start.3 = (bf16[160,256]{1,0:T(8,128)(2,1)S(1)}, bf16[160,256]{1,0:T(8,128)(2,1)S(1)}, u32[]{:S(2)}, u32[]{:S(2)}) collective-permute-start(bf16[160,256]{1,0:T(8,128)(2,1)S(1)} %sum.1.refs_0_), channel_id=1, source_target_pairs={{0,8},{1,3},{2,10},{3,1},{4,12},{5,7},{6,14},{7,5},{8,0},{9,11},{1... | collective-permute-start | bytes 245768 | tf_op jit(solution)/shard_map/ppermute | solution.py:323
  15.7 2.6 %collective-permute-start.4 = (bf16[160,256]{1,0:T(8,128)(2,1)S(1)}, bf16[160,256]{1,0:T(8,128)(2,1)S(1)}, u32[]{:S(2)}, u32[]{:S(2)}) collective-permute-start(bf16[160,256]{1,0:T(8,128)(2,1)S(1)} %sum.1.refs_0_), channel_id=1, source_target_pairs={{0,16},{1,5},{2,18},{3,7},{4,20},{5,1},{6,22},{7,3},{8,24},{9,13},... | collective-permute-start | bytes 245768 | tf_op jit(solution)/shard_map/ppermute | solution.py:323
  18.3 0.2 collective-permute-start.5
  19.2 0.0 copy-done.1
  19.2 1.3 %ready.1 = (f32[20,64,1024]{2,1,0:T(8,128)S(1)}, bf16[128,2048]{1,0:T(8,128)(2,1)S(1)}) custom-call(s32[1,16]{1,0:T(1,128)} %lists_in.1, s32[1,1]{1,0:T(1,128)} %bitcast.2.live, bf16[128,2048]{1,0:T(8,128)(2,1)} %slab.1, f32[1,1024]{1,0:T(1,128)S(1)} %bitcast.3, bf16[20,64,1024]{2,1,0:T(8,128)(2,1)S(1)} %get-tuple-element.11.amps), custom_call_target="tpu_custom_call" | custom-call | tf_op jit(solution)/shard_map/ready/pallas_call | solution.py:285
  20.5 0.0 collective-permute-done.3.refs_1_
  20.5 1.4 %collective-permute-done.4.refs_2_ = bf16[160,256]{1,0:T(8,128)(2,1)S(1)} collective-permute-done((bf16[160,256]{1,0:T(8,128)(2,1)S(1)}, bf16[160,256]{1,0:T(8,128)(2,1)S(1)}, u32[]{:S(2)}, u32[]{:S(2)}) %collective-permute-start.4) | collective-permute-done | bytes 81952 | tf_op jit(solution)/shard_map/ppermute | solution.py:323
  21.9 2.6 %collective-permute-done.5.refs_3_ = bf16[160,256]{1,0:T(8,128)(2,1)S(1)} collective-permute-done((bf16[160,256]{1,0:T(8,128)(2,1)S(1)}, bf16[160,256]{1,0:T(8,128)(2,1)S(1)}, u32[]{:S(2)}, u32[]{:S(2)}) %collective-permute-start.5) | collective-permute-done | bytes 81952 | tf_op jit(solution)/shard_map/ppermute | solution.py:323
  24.5 0.4 %raw.1 = bf16[32,20,128]{2,1,0:T(8,128)(2,1)S(1)} custom-call(bf16[128,2048]{1,0:T(8,128)(2,1)S(1)} %get-tuple-element.12.slab, bf16[160,256]{1,0:T(8,128)(2,1)S(1)} %sum.1.refs_0_, bf16[160,256]{1,0:T(8,128)(2,1)S(1)} %collective-permute-done.3.refs_1_, bf16[160,256]{1,0:T(8,128)(2,1)S(1)} %collective-permute-done.4.refs_2_, ...), custom_call_target="tpu_custom_call" | custom-call | tf_op jit(solution)/shard_map/raw/pallas_call | solution.py:337
  25.0 10.7 %all_to_all.5.raws = bf16[32,20,128]{2,1,0:T(8,128)(2,1)S(1)} all-to-all(bf16[32,20,128]{2,1,0:T(8,128)(2,1)S(1)} %raw.1), channel_id=1, replica_groups=mesh['sp'=16,'pb'=2] {'sp','pb'}, dimensions={0} | all-to-all | bytes 327680 | tf_op jit(solution)/shard_map/all_to_all | solution.py:347
  35.6 0.0 copy-done
  35.6 2.3 %residual.1 = bf16[20,64,1024]{2,1,0:T(8,128)(2,1)} custom-call(bf16[32,20,128]{2,1,0:T(8,128)(2,1)S(1)} %all_to_all.5.raws, bf16[20,40]{1,0:T(8,128)(2,1)S(1)} %copy-done, bf16[2,64,64]{2,1,0:T(8,128)(2,1)S(1)} %get-tuple-element.14.left, bf16[256,1024]{1,0:T(8,128)(2,1)S(1)} %get-tuple-element.15.right, f32[20,64,1024]{2,1,0:T(8,128)S(1)} %get-tuple-element.16.product), custom_call_target="tpu_custom_call" | custom-call | tf_op jit(solution)/shard_map/residual/pallas_call | solution.py:348
  (1 shorter events, 0.0 us)
Async XLA Ops:
  0.0 19.2 %copy-start.1 = (f32[1024]{0:T(1024)S(1)}, f32[1024]{0:T(1024)}, u32[]{:S(2)}) copy-start(f32[1024]{0:T(1024)} %param.10) | copy-start | bytes 12292
  4.1 31.5 %copy-start = (bf16[20,40]{1,0:T(8,128)(2,1)S(1)}, bf16[20,40]{1,0:T(8,128)(2,1)}, u32[]{:S(2)}) copy-start(bf16[20,40]{1,0:T(8,128)(2,1)} %coupling.1) | copy-start | bytes 4804
  4.1 5.5 %collective-permute-start = (bf16[160,256]{1,0:T(8,128)(2,1)S(1)}, bf16[160,256]{1,0:T(8,128)(2,1)S(1)}, u32[]{:S(2)}, u32[]{:S(2)}) collective-permute-start(bf16[160,256]{1,0:T(8,128)(2,1)S(1)} %get-tuple-element.13.refs_0_), channel_id=1, source_target_pairs={{0,2},{1,9},{2,0},{3,11},{4,6},{5,13},{6,4},{7,15},{8,10},{9,1},{1... | collective-permute-start | bytes 245768 | tf_op jit(solution)/shard_map/ppermute | solution.py:323
  7.2 4.4 %collective-permute-start.1 = (bf16[160,256]{1,0:T(8,128)(2,1)S(1)}, bf16[160,256]{1,0:T(8,128)(2,1)S(1)}, u32[]{:S(2)}, u32[]{:S(2)}) collective-permute-start(bf16[160,256]{1,0:T(8,128)(2,1)S(1)} %get-tuple-element.13.refs_0_), channel_id=1, source_target_pairs={{0,4},{1,17},{2,6},{3,19},{4,0},{5,21},{6,2},{7,23},{8,12},{9,25},... | collective-permute-start | bytes 245768 | tf_op jit(solution)/shard_map/ppermute | solution.py:323
  8.7 5.3 %collective-permute-start.2 = (bf16[160,256]{1,0:T(8,128)(2,1)S(1)}, bf16[160,256]{1,0:T(8,128)(2,1)S(1)}, u32[]{:S(2)}, u32[]{:S(2)}) collective-permute-start(bf16[160,256]{1,0:T(8,128)(2,1)S(1)} %get-tuple-element.13.refs_0_), channel_id=1, source_target_pairs={{0,6},{1,25},{2,4},{3,27},{4,2},{5,29},{6,0},{7,31},{8,14},{9,17},... | collective-permute-start | bytes 245768 | tf_op jit(solution)/shard_map/ppermute | solution.py:323
  14.1 6.4 %collective-permute-start.3 = (bf16[160,256]{1,0:T(8,128)(2,1)S(1)}, bf16[160,256]{1,0:T(8,128)(2,1)S(1)}, u32[]{:S(2)}, u32[]{:S(2)}) collective-permute-start(bf16[160,256]{1,0:T(8,128)(2,1)S(1)} %sum.1.refs_0_), channel_id=1, source_target_pairs={{0,8},{1,3},{2,10},{3,1},{4,12},{5,7},{6,14},{7,5},{8,0},{9,11},{1... | collective-permute-start | bytes 245768 | tf_op jit(solution)/shard_map/ppermute | solution.py:323
  15.7 6.2 %collective-permute-start.4 = (bf16[160,256]{1,0:T(8,128)(2,1)S(1)}, bf16[160,256]{1,0:T(8,128)(2,1)S(1)}, u32[]{:S(2)}, u32[]{:S(2)}) collective-permute-start(bf16[160,256]{1,0:T(8,128)(2,1)S(1)} %sum.1.refs_0_), channel_id=1, source_target_pairs={{0,16},{1,5},{2,18},{3,7},{4,20},{5,1},{6,22},{7,3},{8,24},{9,13},... | collective-permute-start | bytes 245768 | tf_op jit(solution)/shard_map/ppermute | solution.py:323
  18.3 6.2 %collective-permute-start.5 = (bf16[160,256]{1,0:T(8,128)(2,1)S(1)}, bf16[160,256]{1,0:T(8,128)(2,1)S(1)}, u32[]{:S(2)}, u32[]{:S(2)}) collective-permute-start(bf16[160,256]{1,0:T(8,128)(2,1)S(1)} %sum.1.refs_0_), channel_id=1, source_target_pairs={{0,24},{1,7},{2,26},{3,5},{4,28},{5,3},{6,30},{7,1},{8,16},{9,15},... | collective-permute-start | bytes 245768 | tf_op jit(solution)/shard_map/ppermute | solution.py:323
